TPU v7x, 32 devices: a whole 2x2x4 slice. The times are simulated.
32 devices in a mesh: parts: 2 (over y), space: 4 (over z), filt: 2 (over x), rep: 2 (over core).
Axes of the slice: x: 2, y: 2, z: 4, core: 2. Of those that a mesh axis runs over, the one named last changes fastest.
Arguments:
- features: bfloat16 [128, 512, 256], P(('parts', 'space'), 'filt', 'rep'), parts along dimension 0, may hold values from -6 to 6
- kernel: bfloat16 [3, 3, 512, 512], P(None, None, 'filt'), may hold values from -0.09375 to 0.09375
- shift_bias: float32 [512], P('filt'), may hold values from -3 to 3
- upstream: bfloat16 [128, 512, 256], P(('parts', 'space'), 'filt', 'rep'), parts along dimension 0, may hold values from -6 to 6
Outputs:
- block_out: bfloat16 [128, 512, 256], P(('parts', 'space'), 'filt', 'rep'), parts along dimension 0
- input_grad: bfloat16 [128, 512, 256], P(('parts', 'space'), 'filt', 'rep'), parts along dimension 0
- kernel_grad: float32 [6, 3, 512, 512], P('parts', None, 'filt'), parts along dimension 0
- bias_grad: float32 [1024], P(('parts', 'filt')), parts along dimension 0
There are 2 independent parts, one for each index of `parts`. A program takes and returns all parts, laid end to end along the dimension named above; an argument that names none is the same for every part. Nothing has to cross between parts.
All inputs are finite; a program needn't handle non-finite values.
Results may differ from a plain program's by a relative error of at most 0.0055.
Values may be sent and summed in bfloat16 or wider, within the bound.
No kernel may reach another device: no remote copies, remote signals or barrier semaphores. Data moves between devices by JAX's collectives and lax.ppermute only.
A program may use at most 64 MiB of HBM per device.

v0:
```python
import jax
import jax.numpy as jnp
from jax import lax
from jax.sharding import PartitionSpec as P


def padded(cells, sides, width):
    for axis, dim in sides:
        count = lax.axis_size(axis)
        ends = count - 1
        head = lax.slice_in_dim(cells, 0, width, axis=dim)
        tail = lax.slice_in_dim(cells, cells.shape[dim] - width, cells.shape[dim], axis=dim)
        cells = jnp.concatenate(
            [
                lax.ppermute(tail, axis, [(i, (i + 1) % count) for i in range(ends)]),
                cells,
                lax.ppermute(head, axis, [((i + 1) % count, i) for i in range(ends)]),
            ],
            axis=dim,
        )
    return cells


def forward_taps(running, panels, kernel, band_rows, band_cols):
    for row_tap in range(3):
        for col_tap in range(3):
            window = panels[row_tap : row_tap + band_rows, :, col_tap : col_tap + band_cols]
            weights = kernel[row_tap, col_tap]
            running = running + jnp.einsum(
                "oc,hcw->how", weights, window, preferred_element_type=jnp.float32
            )
    return running


def weight_taps(panels, slope, band_rows, band_cols):
    rows_out = []
    for row_tap in range(3):
        taps_row = []
        for col_tap in range(3):
            window = panels[row_tap : row_tap + band_rows, :, col_tap : col_tap + band_cols]
            taps_row.append(
                jnp.einsum("how,hcw->oc", slope, window, preferred_element_type=jnp.float32)
            )
        rows_out.append(jnp.stack(taps_row))
    return jnp.stack(rows_out)


def backward_taps(slope_pad, weights, band_rows, band_cols):
    summed = jnp.zeros((band_rows, weights.shape[3], band_cols), jnp.float32)
    for row_tap in range(3):
        for col_tap in range(3):
            part_slope = slope_pad[
                2 - row_tap : 2 - row_tap + band_rows, :, 2 - col_tap : 2 - col_tap + band_cols
            ]
            summed = summed + jnp.einsum(
                "oc,how->hcw",
                weights[row_tap, col_tap],
                part_slope,
                preferred_element_type=jnp.float32,
            )
    return summed


def per_device(features, kernel, shift_bias, upstream):
    band_rows, local_out, band_cols = upstream.shape
    rimmed = padded(features, (("space", 0), ("rep", 2)), 1)
    start_pre = (
        jnp.zeros((band_rows, local_out, band_cols), jnp.float32) + shift_bias[None, :, None]
    )
    all_panels = lax.all_gather(rimmed, "filt", axis=1, tiled=True)
    pre = forward_taps(start_pre, all_panels, kernel, band_rows, band_cols)
    sigm = jax.nn.sigmoid(pre)
    block_out = (features.astype(jnp.float32) + pre * sigm).astype(jnp.bfloat16)
    slope = (upstream.astype(jnp.float32) * sigm * (1.0 + pre * (1.0 - sigm))).astype(jnp.bfloat16)
    kernel_part = weight_taps(all_panels, slope, band_rows, band_cols)
    slope_pad = padded(slope, (("space", 0), ("rep", 2)), 1)
    slope_all = lax.all_gather(slope_pad, "filt", axis=1, tiled=True)
    own_rows = lax.all_to_all(kernel, "filt", split_axis=3, concat_axis=2, tiled=True)
    back = backward_taps(slope_all, own_rows, band_rows, band_cols)
    input_grad = (upstream.astype(jnp.float32) + back).astype(jnp.bfloat16)
    bias_part = jnp.sum(slope.astype(jnp.float32), axis=(0, 2))
    kernel_sum, bias_sum = lax.psum((kernel_part, bias_part), ("space", "rep"))
    total_cells = band_rows * band_cols * lax.axis_size("space") * lax.axis_size("rep")
    scale = 1.0 / jnp.sqrt(jnp.float32(total_cells))
    return (block_out, input_grad, kernel_sum * scale, bias_sum * scale)


def solution(mesh):
    in_specs = (
        P(("parts", "space"), "filt", "rep"),
        P(None, None, "filt", None),
        P("filt"),
        P(("parts", "space"), "filt", "rep"),
    )
    out_specs = (
        P(("parts", "space"), "filt", "rep"),
        P(("parts", "space"), "filt", "rep"),
        P("parts", None, "filt", None),
        P(("parts", "filt")),
    )
    return jax.shard_map(
        per_device, mesh=mesh, in_specs=in_specs, out_specs=out_specs, check_vma=False
    )
```

profile of v0, /device:TPU:0, one launch (start us, length us, event | category | flops | bytes accessed | tf_op | source)
XLA Modules:
  0.0 250.9 jit_solution(6216047578776951642)
XLA Ops:
  7.2 1.5 copy.34
  8.7 1.3 collective-permute-start.1
  10.0 5.6 %collective-permute-start = (bf16[1,256,128]{1,2,0:T(8,128)(2,1)S(1)}, bf16[1,256,128]{1,2,0:T(8,128)(2,1)S(1)}, u32[]{:S(2)}, u32[]{:S(2)}) collective-permute-start(bf16[1,256,128]{1,2,0:T(8,128)(2,1)S(1)} %get-tuple-element.21), channel_id=1, source_target_pairs={{0,4},{4,8},{8,12},{1,5},{5,9},{9,13},{2,6},{6,10},{10,14},{3,7},{... | collective-permute-start | bytes 196616 | tf_op jit(solution)/shard_map/ppermute | solution.py:15
  15.9 1.6 collective-permute-done
  17.6 1.4 collective-permute-start.3
  19.0 3.0 %collective-permute-start.2 = (bf16[18,256,1]{1,2,0:T(2,128)(2,1)S(1)}, bf16[18,256,1]{1,2,0:T(2,128)(2,1)S(1)}, u32[]{:S(2)}, u32[]{:S(2)}) collective-permute-start(bf16[18,256,1]{1,2,0:T(2,128)(2,1)S(1)} %get-tuple-element.17), channel_id=1, source_target_pairs={{0,1},{2,3},{4,5},{6,7},{8,9},{10,11},{12,13},{14,15},{16,17},{18,... | collective-permute-start | bytes 27656 | tf_op jit(solution)/shard_map/ppermute | solution.py:15
  22.0 0.8 collective-permute-done.2
  22.8 1.7 pad_maximum_fusion.1
  25.2 39.7 %all-gather.3.cloned.1.call-done = bf16[18,512,130]{1,2,0:T(8,128)(2,1)} async-done(((bf16[18,256,130]{1,2,0:T(8,128)(2,1)}), bf16[18,512,130]{1,2,0:T(8,128)(2,1)}) %all-gather.3.cloned.1.call-update) | async-done | bytes 2396176 | tf_op jit(solution)/shard_map/all_gather | solution.py:70
  64.9 2.5 %fusion.33 = f32[16,128,256]{2,1,0:T(8,128)S(1)} fusion(bf16[18,512,130]{1,2,0:T(8,128)(2,1)} %all-gather.3.cloned.1.call-done, bf16[3,3,256,512]{3,2,1,0:T(8,128)(2,1)} %param.5), kind=kOutput, calls=%fused_computation.42 | convolution fusion | flops 536870912 | bytes 4456448 | tf_op jit(solution)/shard_map/oc,hcw->how/dot_general | solution.py:29
  73.4 3.4 %convert_reduce_fusion = (f32[256]{0:T(256)S(1)}, bf16[16,256,128]{1,2,0:T(8,128)(2,1)S(1)}, bf16[16,256,128]{1,2,0:T(8,128)(2,1)}) fusion(bf16[16,256,128]{1,2,0:T(8,128)(2,1)S(1)} %copy.38, bf16[16,256,128]{1,2,0:T(8,128)(2,1)S(1)} %copy.34, bf16[3,3,256,512]{3,2,1,0:T(8,128)(2,1)S(1)} %copy-done.2, bf16[18,512,130]{1,2,0:T(8,128)(2,1)S(1)} %copy-done, ...), kind=kOutput, calls=%fused_computation.35 | convolution fusion | flops 549977856 | bytes 23332864 | tf_op jit(solution)/shard_map/oc,hcw->how/dot_general | solution.py:29
  77.6 0.8 fusion.88
  79.2 0.8 fusion.73
  84.3 2.7 %pad_maximum_fusion = f32[3,3,256,512]{3,2,1,0:T(8,128)} fusion(f32[1,3,256,512]{3,2,1,0:T(8,128)S(1)} %maximum_bitcast_fusion.2, f32[1,3,256,512]{3,2,1,0:T(8,128)S(1)} %get-tuple-element.24, f32[1,3,256,512]{3,2,1,0:T(8,128)S(1)} %get-tuple-element.23), kind=kLoop, calls=%fused_computation | loop fusion | flops 2359296 | bytes 9437184 | tf_op jit(solution)/shard_map/stack | solution.py:45
  87.1 1.3 collective-permute-start.5
  88.4 4.5 %collective-permute-start.4 = (bf16[1,256,128]{1,2,0:T(8,128)(2,1)S(1)}, bf16[1,256,128]{1,2,0:T(8,128)(2,1)S(1)}, u32[]{:S(2)}, u32[]{:S(2)}) collective-permute-start(bf16[1,256,128]{1,2,0:T(8,128)(2,1)S(1)} %get-tuple-element.19), channel_id=1, source_target_pairs={{0,4},{4,8},{8,12},{1,5},{5,9},{9,13},{2,6},{6,10},{10,14},{3,7},{... | collective-permute-start | bytes 196616 | tf_op jit(solution)/shard_map/ppermute | solution.py:15
  93.3 3.0 %collective-permute-done.4 = bf16[1,256,128]{1,2,0:T(8,128)(2,1)S(1)} collective-permute-done((bf16[1,256,128]{1,2,0:T(8,128)(2,1)S(1)}, bf16[1,256,128]{1,2,0:T(8,128)(2,1)S(1)}, u32[]{:S(2)}, u32[]{:S(2)}) %collective-permute-start.4) | collective-permute-done | bytes 65568 | tf_op jit(solution)/shard_map/ppermute | solution.py:15
  96.4 1.4 collective-permute-start.7
  97.8 3.0 %collective-permute-start.6 = (bf16[18,256,1]{1,2,0:T(2,128)(2,1)S(1)}, bf16[18,256,1]{1,2,0:T(2,128)(2,1)S(1)}, u32[]{:S(2)}, u32[]{:S(2)}) collective-permute-start(bf16[18,256,1]{1,2,0:T(2,128)(2,1)S(1)} %get-tuple-element.15), channel_id=1, source_target_pairs={{0,1},{2,3},{4,5},{6,7},{8,9},{10,11},{12,13},{14,15},{16,17},{18,... | collective-permute-start | bytes 27656 | tf_op jit(solution)/shard_map/ppermute | solution.py:15
  100.8 0.8 collective-permute-done.6
  101.7 1.7 pad_maximum_fusion.2
  103.4 3.8 %copy.39 = bf16[3,3,256,512]{2,1,0,3:T(4,128)(2,1)} copy(bf16[3,3,256,512]{3,2,1,0:T(8,128)(2,1)S(1)} %copy-done.3) | data formatting | bytes 4718592 | tf_op args[1]
  107.2 40.8 %all_to_all.18 = bf16[3,3,256,512]{2,1,0,3:T(4,128)(2,1)S(1)} all-to-all(bf16[3,3,256,512]{2,1,0,3:T(4,128)(2,1)} %copy.39), channel_id=1, replica_groups=mesh['parts'=2,'space'=4,'filt'=2,'rep'=2] {'filt'}, dimensions={3} | all-to-all | bytes 4718592 | tf_op jit(solution)/shard_map/all_to_all | solution.py:78
  148.0 3.6 %copy.40 = bf16[3,3,256,2,256]{4,2,3,1,0:T(8,128)(2,1)} copy(bf16[3,3,256,2,256]{2,1,0,4,3:T(4,128)(2,1)S(1)} %bitcast.163) | data formatting | bytes 4718592 | tf_op jit(solution)/shard_map/all_to_all | solution.py:78
  151.6 2.3 copy.59
  153.9 17.7 %psum.15 = f32[256]{0:T(256)S(1)} all-reduce(f32[256]{0:T(256)S(1)} %get-tuple-element.12), channel_id=1, replica_groups=mesh['parts'=2,'space'=4,'filt'=2,'rep'=2] {'space','rep'}, use_global_device_ids=true, to_apply=%region_2.0 | all-reduce | flops 256 | bytes 2048 | tf_op jit(solution)/shard_map/psum | solution.py:82
  172.1 22.5 %all-reduce.2.cloned.1.call-done = f32[3,3,256,512]{3,2,1,0:T(8,128)} async-done(((f32[3,3,256,512]{3,2,1,0:T(8,128)}), f32[3,3,256,512]{3,2,1,0:T(8,128)}) %all-reduce.2.cloned.1.call-update) | async-done | bytes 4718608 | tf_op jit(solution)/shard_map/psum | solution.py:82
  194.6 5.3 %broadcast_multiply_fusion = f32[3,3,256,512]{3,2,1,0:T(8,128)} fusion(f32[3,3,256,512]{3,2,1,0:T(8,128)} %all-reduce.2.cloned.1.call-done), kind=kLoop, calls=%fused_computation.3 | loop fusion | flops 1179648 | bytes 9437184 | tf_op jit(solution)/shard_map/mul | solution.py:85
  199.9 34.0 %all-gather.5.cloned.1.call-done = bf16[18,512,130]{1,2,0:T(8,128)(2,1)} async-done(((bf16[18,256,130]{1,2,0:T(8,128)(2,1)}), bf16[18,512,130]{1,2,0:T(8,128)(2,1)}) %all-gather.5.cloned.1.call-update) | async-done | bytes 2396176 | tf_op jit(solution)/shard_map/all_gather | solution.py:77
  233.9 2.5 fusion.5
  242.0 1.1 fusion.2
  243.1 1.3 copy.60
  (57 shorter events, 19.3 us)
Async XLA Ops:
  7.2 57.7 %all-gather.3.cloned.1.call-start = ((), (), s32[]{:S(2)}) async-start(), calls=%async_computation.1 | async-start | bytes 3760128 | tf_op jit(solution)/shard_map/all_gather | solution.py:70
  8.7 7.2 %collective-permute-start.1 = (bf16[1,256,128]{1,2,0:T(8,128)(2,1)S(1)}, bf16[1,256,128]{1,2,0:T(8,128)(2,1)S(1)}, u32[]{:S(2)}, u32[]{:S(2)}) collective-permute-start(bf16[1,256,128]{1,2,0:T(8,128)(2,1)S(1)} %get-tuple-element.22), channel_id=1, source_target_pairs={{4,0},{8,4},{12,8},{5,1},{9,5},{13,9},{6,2},{10,6},{14,10},{7,3},{... | collective-permute-start | bytes 196616 | tf_op jit(solution)/shard_map/ppermute | solution.py:17
  10.0 7.5 %collective-permute-start = (bf16[1,256,128]{1,2,0:T(8,128)(2,1)S(1)}, bf16[1,256,128]{1,2,0:T(8,128)(2,1)S(1)}, u32[]{:S(2)}, u32[]{:S(2)}) collective-permute-start(bf16[1,256,128]{1,2,0:T(8,128)(2,1)S(1)} %get-tuple-element.21), channel_id=1, source_target_pairs={{0,4},{4,8},{8,12},{1,5},{5,9},{9,13},{2,6},{6,10},{10,14},{3,7},{... | collective-permute-start | bytes 196616 | tf_op jit(solution)/shard_map/ppermute | solution.py:15
  17.5 7.1 %copy-start.7 = (bf16[16,256,128]{2,1,0:T(8,128)(2,1)S(1)}, bf16[16,256,128]{2,1,0:T(8,128)(2,1)}, u32[]{:S(2)}) copy-start(bf16[16,256,128]{2,1,0:T(8,128)(2,1)} %param.7) | copy-start | bytes 3145732
  17.6 4.5 %collective-permute-start.3 = (bf16[18,256,1]{1,2,0:T(2,128)(2,1)S(1)}, bf16[18,256,1]{1,2,0:T(2,128)(2,1)S(1)}, u32[]{:S(2)}, u32[]{:S(2)}) collective-permute-start(bf16[18,256,1]{1,2,0:T(2,128)(2,1)S(1)} %get-tuple-element.18), channel_id=1, source_target_pairs={{1,0},{3,2},{5,4},{7,6},{9,8},{11,10},{13,12},{15,14},{17,16},{19,... | collective-permute-start | bytes 27656 | tf_op jit(solution)/shard_map/ppermute | solution.py:17
  19.0 3.9 %collective-permute-start.2 = (bf16[18,256,1]{1,2,0:T(2,128)(2,1)S(1)}, bf16[18,256,1]{1,2,0:T(2,128)(2,1)S(1)}, u32[]{:S(2)}, u32[]{:S(2)}) collective-permute-start(bf16[18,256,1]{1,2,0:T(2,128)(2,1)S(1)} %get-tuple-element.17), channel_id=1, source_target_pairs={{0,1},{2,3},{4,5},{6,7},{8,9},{10,11},{12,13},{14,15},{16,17},{18,... | collective-permute-start | bytes 27656 | tf_op jit(solution)/shard_map/ppermute | solution.py:15
  24.6 170.0 %all-reduce.2.cloned.1.call-start = ((), (), s32[]{:S(2)}) async-start(), calls=%async_computation.3 | async-start | bytes 9437184 | tf_op jit(solution)/shard_map/psum | solution.py:82
  25.2 48.2 %copy-start.5 = (bf16[16,256,128]{1,2,0:T(8,128)(2,1)}, bf16[16,256,128]{1,2,0:T(8,128)(2,1)S(1)}, u32[]{:S(2)}) copy-start(bf16[16,256,128]{1,2,0:T(8,128)(2,1)S(1)} %copy.38) | copy-start | bytes 3145732
  64.9 2.5 %copy-start = (bf16[18,512,130]{1,2,0:T(8,128)(2,1)S(1)}, bf16[18,512,130]{1,2,0:T(8,128)(2,1)}, u32[]{:S(2)}) copy-start(bf16[18,512,130]{1,2,0:T(8,128)(2,1)} %all-gather.3.cloned.1.call-done) | copy-start | bytes 7188484
  64.9 3.2 %copy-start.2 = (bf16[3,3,256,512]{3,2,1,0:T(8,128)(2,1)S(1)}, bf16[3,3,256,512]{3,2,1,0:T(8,128)(2,1)}, u32[]{:S(2)}) copy-start(bf16[3,3,256,512]{3,2,1,0:T(8,128)(2,1)} %param.5) | copy-start | bytes 7077892
  72.6 0.8 copy-start.8
  87.1 146.9 %all-gather.5.cloned.1.call-start = ((), (), s32[]{:S(2)}) async-start(), calls=%async_computation.2 | async-start | bytes 3760128 | tf_op jit(solution)/shard_map/all_gather | solution.py:77
  87.1 6.2 %collective-permute-start.5 = (bf16[1,256,128]{1,2,0:T(8,128)(2,1)S(1)}, bf16[1,256,128]{1,2,0:T(8,128)(2,1)S(1)}, u32[]{:S(2)}, u32[]{:S(2)}) collective-permute-start(bf16[1,256,128]{1,2,0:T(8,128)(2,1)S(1)} %get-tuple-element.20), channel_id=1, source_target_pairs={{4,0},{8,4},{12,8},{5,1},{9,5},{13,9},{6,2},{10,6},{14,10},{7,3},{... | collective-permute-start | bytes 196616 | tf_op jit(solution)/shard_map/ppermute | solution.py:17
  88.4 7.9 %collective-permute-start.4 = (bf16[1,256,128]{1,2,0:T(8,128)(2,1)S(1)}, bf16[1,256,128]{1,2,0:T(8,128)(2,1)S(1)}, u32[]{:S(2)}, u32[]{:S(2)}) collective-permute-start(bf16[1,256,128]{1,2,0:T(8,128)(2,1)S(1)} %get-tuple-element.19), channel_id=1, source_target_pairs={{0,4},{4,8},{8,12},{1,5},{5,9},{9,13},{2,6},{6,10},{10,14},{3,7},{... | collective-permute-start | bytes 196616 | tf_op jit(solution)/shard_map/ppermute | solution.py:15
  96.4 7.1 %copy-start.3 = (bf16[3,3,256,512]{3,2,1,0:T(8,128)(2,1)S(1)}, bf16[3,3,256,512]{3,2,1,0:T(8,128)(2,1)}, u32[]{:S(2)}) copy-start(bf16[3,3,256,512]{3,2,1,0:T(8,128)(2,1)} %param.5) | copy-start | bytes 7077892
  96.4 4.5 %collective-permute-start.7 = (bf16[18,256,1]{1,2,0:T(2,128)(2,1)S(1)}, bf16[18,256,1]{1,2,0:T(2,128)(2,1)S(1)}, u32[]{:S(2)}, u32[]{:S(2)}) collective-permute-start(bf16[18,256,1]{1,2,0:T(2,128)(2,1)S(1)} %get-tuple-element.16), channel_id=1, source_target_pairs={{1,0},{3,2},{5,4},{7,6},{9,8},{11,10},{13,12},{15,14},{17,16},{19,... | collective-permute-start | bytes 27656 | tf_op jit(solution)/shard_map/ppermute | solution.py:17
  97.8 3.9 %collective-permute-start.6 = (bf16[18,256,1]{1,2,0:T(2,128)(2,1)S(1)}, bf16[18,256,1]{1,2,0:T(2,128)(2,1)S(1)}, u32[]{:S(2)}, u32[]{:S(2)}) collective-permute-start(bf16[18,256,1]{1,2,0:T(2,128)(2,1)S(1)} %get-tuple-element.15), channel_id=1, source_target_pairs={{0,1},{2,3},{4,5},{6,7},{8,9},{10,11},{12,13},{14,15},{16,17},{18,... | collective-permute-start | bytes 27656 | tf_op jit(solution)/shard_map/ppermute | solution.py:15
  172.1 61.8 %copy-start.4 = (bf16[3,3,256,2,256]{4,2,3,1,0:T(8,128)(2,1)S(1)}, bf16[3,3,256,2,256]{4,2,3,1,0:T(8,128)(2,1)}, u32[]{:S(2)}) copy-start(bf16[3,3,256,2,256]{4,2,3,1,0:T(8,128)(2,1)} %copy.40) | copy-start | bytes 7077892
  233.9 2.5 copy-start.1
  240.8 1.2 copy-start.6
Sparse Core Ops, SparseCore 0:
  24.7 40.1 all-gather.2
  87.2 107.3 all-reduce.1
  196.2 37.7 all-gather.4
where the time goes:
time: 251 us
  waiting for transfers between devices  103 us (41%)
  blocking collectives  58.5 us (23%)
  matrix products  26.5 us (11%)
  starting transfers between devices  21.7 us (9%)
  local copies, waits for them, and re-layouts  14.2 us (6%)
  between operations  14.2 us (6%)
  other arithmetic  12.8 us (5%)
    all_to_all x1, blocking collectives, per_device(): lax.all_to_all(kernel, 'filt', split_axis=3, concat_axis=2, tiled=True)  40.8 us
    all_gather x1, waiting for transfers between devices, per_device(): all_panels = lax.all_gather(rimmed, 'filt', axis=1, tiled=True)  39.7 us
    all_gather x1, waiting for transfers between devices, per_device(): slope_all = lax.all_gather(slope_pad, 'filt', axis=1, tiled=True)  34 us
    psum x1, waiting for transfers between devices, per_device(): kernel_sum, bias_sum = lax.psum((kernel_part, bias_part), ('space', 'rep'))  22.5 us
    psum x1, blocking collectives, per_device(): kernel_sum, bias_sum = lax.psum((kernel_part, bias_part), ('space', 'rep'))  17.7 us
    ppermute x4, starting transfers between devices, padded(): lax.ppermute(tail, axis, [(i, (i + 1) % count) for i in range(ends)])  16.2 us
    dot_general x9, matrix products, forward_taps(): jnp.einsum('oc,hcw->how', weights, window, preferred_element_type=jnp.flo...  11.2 us
    unnamed x23, local copies, waits for them, and re-layouts  10.5 us
  transfers between devices with their start and end apart: 11, of which 9 were waited for; matrix products, arithmetic and copies ran while one was open for 7% of the time, Pallas kernels for 0%

commit v1 on v0

--- a/solution.py
+++ b/solution.py
@@ -79,7 +79,9 @@
     back = backward_taps(slope_all, own_rows, band_rows, band_cols)
     input_grad = (upstream.astype(jnp.float32) + back).astype(jnp.bfloat16)
     bias_part = jnp.sum(slope.astype(jnp.float32), axis=(0, 2))
-    kernel_sum, bias_sum = lax.psum((kernel_part, bias_part), ("space", "rep"))
+    kernel_sum, bias_sum = jax.lax.psum(
+        jax.lax.psum((kernel_part, bias_part), axis_name="rep"), axis_name="space"
+    )
     total_cells = band_rows * band_cols * lax.axis_size("space") * lax.axis_size("rep")
     scale = 1.0 / jnp.sqrt(jnp.float32(total_cells))
     return (block_out, input_grad, kernel_sum * scale, bias_sum * scale)

time: 251 us -> 361 us (1.44)
  waiting for transfers between devices: 103 us -> 251 us
  blocking collectives: 58.5 us -> 15.8 us
  starting transfers between devices: 21.7 us -> 26.1 us
    psum x1 -> x2, waiting for transfers between devices: 22.5 us -> 157 us  [the longest x1 151 us: per_device(): jax.lax.psum(jax.lax.psum((kernel_part, bias_part), axis_name='rep'), axi...]
    all_to_all x0 -> x1, waiting for transfers between devices: none -> 48.8 us  [per_device(): lax.all_to_all(kernel, 'filt', split_axis=3, concat_axis=2, tiled=True)]
    all_to_all x1 -> x0, blocking collectives: 40.8 us -> none  [per_device(): lax.all_to_all(kernel, 'filt', split_axis=3, concat_axis=2, tiled=True)]
    all_gather x1, waiting for transfers between devices: 34 us -> 0.01 us  [per_device(): slope_all = lax.all_gather(slope_pad, 'filt', axis=1, tiled=True)]
    all_to_all x0 -> x1, starting transfers between devices: none -> 4.21 us  [per_device(): lax.all_to_all(kernel, 'filt', split_axis=3, concat_axis=2, tiled=True)]
    psum x1 -> x2, blocking collectives: 17.7 us -> 15.8 us  [the longest x1 13.3 us: per_device(): jax.lax.psum(jax.lax.psum((kernel_part, bias_part), axis_name='rep'), axi...]
  transfers between devices with their start and end apart: 11 -> 13, of which waited for: 9 -> 10; matrix products, arithmetic and copies ran while one was open for 7% -> 6% of each run, Pallas kernels for 0% -> 0%
where the time goes in v1:
time: 361 us
  waiting for transfers between devices  251 us (70%)
  matrix products  26.5 us (7%)
  starting transfers between devices  26.1 us (7%)
  blocking collectives  15.8 us (4%)
  local copies, waits for them, and re-layouts  14.8 us (4%)
  between operations  14.2 us (4%)
  other arithmetic  12.8 us (4%)
    psum x1, waiting for transfers between devices, per_device(): jax.lax.psum(jax.lax.psum((kernel_part, bias_part), axis_name='rep'), axi...  151 us
    all_to_all x1, waiting for transfers between devices, per_device(): lax.all_to_all(kernel, 'filt', split_axis=3, concat_axis=2, tiled=True)  48.8 us
    all_gather x1, waiting for transfers between devices, per_device(): all_panels = lax.all_gather(rimmed, 'filt', axis=1, tiled=True)  39.7 us
    ppermute x4, starting transfers between devices, padded(): lax.ppermute(tail, axis, [(i, (i + 1) % count) for i in range(ends)])  16.2 us
    psum x1, blocking collectives, per_device(): jax.lax.psum(jax.lax.psum((kernel_part, bias_part), axis_name='rep'), axi...  13.3 us
    dot_general x9, matrix products, forward_taps(): jnp.einsum('oc,hcw->how', weights, window, preferred_element_type=jnp.flo...  11.2 us
    unnamed x23, local copies, waits for them, and re-layouts  11.1 us
    dot_general x9, matrix products, backward_taps(): jnp.einsum('oc,how->hcw', weights[row_tap, col_tap], part_slope, preferre...  8.55 us
  transfers between devices with their start and end apart: 13, of which 10 were waited for; matrix products, arithmetic and copies ran while one was open for 6% of the time, Pallas kernels for 0%

profile of v1, /device:TPU:0, one launch (start us, length us, event | category | flops | bytes accessed | tf_op | source)
XLA Modules:
  0.0 360.9 jit_solution(168119410281818128)
XLA Ops:
  7.2 1.5 copy.34
  8.7 1.3 collective-permute-start.1
  10.0 5.6 %collective-permute-start = (bf16[1,256,128]{1,2,0:T(8,128)(2,1)S(1)}, bf16[1,256,128]{1,2,0:T(8,128)(2,1)S(1)}, u32[]{:S(2)}, u32[]{:S(2)}) collective-permute-start(bf16[1,256,128]{1,2,0:T(8,128)(2,1)S(1)} %get-tuple-element.21), channel_id=1, source_target_pairs={{0,4},{4,8},{8,12},{1,5},{5,9},{9,13},{2,6},{6,10},{10,14},{3,7},{... | collective-permute-start | bytes 196616 | tf_op jit(solution)/shard_map/ppermute | solution.py:15
  15.9 1.6 collective-permute-done
  17.6 1.4 collective-permute-start.3
  19.0 3.0 collective-permute-start.2
  22.0 0.8 collective-permute-done.2
  22.8 1.7 pad_maximum_fusion.1
  25.2 39.7 %all-gather.3.cloned.1.call-done = bf16[18,512,130]{1,2,0:T(8,128)(2,1)} async-done(((bf16[18,256,130]{1,2,0:T(8,128)(2,1)}), bf16[18,512,130]{1,2,0:T(8,128)(2,1)}) %all-gather.3.cloned.1.call-update) | async-done | bytes 2396176 | tf_op jit(solution)/shard_map/all_gather | solution.py:70
  64.9 2.5 fusion.33
  73.4 3.4 convert_reduce_fusion
  84.3 2.7 pad_maximum_fusion
  87.1 1.3 collective-permute-start.5
  88.4 4.5 %collective-permute-start.4 = (bf16[1,256,128]{1,2,0:T(8,128)(2,1)S(1)}, bf16[1,256,128]{1,2,0:T(8,128)(2,1)S(1)}, u32[]{:S(2)}, u32[]{:S(2)}) collective-permute-start(bf16[1,256,128]{1,2,0:T(8,128)(2,1)S(1)} %get-tuple-element.19), channel_id=1, source_target_pairs={{0,4},{4,8},{8,12},{1,5},{5,9},{9,13},{2,6},{6,10},{10,14},{3,7},{... | collective-permute-start | bytes 196616 | tf_op jit(solution)/shard_map/ppermute | solution.py:15
  93.3 1.6 collective-permute-done.4
  94.9 1.6 collective-permute-start.7
  96.5 3.0 collective-permute-start.6
  99.5 0.8 collective-permute-done.6
  100.3 1.8 pad_maximum_fusion.2
  102.1 3.7 %copy.39 = bf16[3,3,256,512]{2,1,0,3:T(4,128)(2,1)} copy(bf16[3,3,256,512]{3,2,1,0:T(8,128)(2,1)S(1)} %copy-done.3) | data formatting | bytes 4718592 | tf_op args[1]
  105.9 4.2 %all-to-all-start = ((bf16[3,3,256,512]{2,1,0,3:T(4,128)(2,1)}), bf16[3,3,256,512]{2,1,0,3:T(4,128)(2,1)S(1)}, u32[]{:S(2)}, u32[]{:S(2)}) async-start(bf16[3,3,256,512]{2,1,0,3:T(4,128)(2,1)} %copy.39), calls=%async_computation | async-start | bytes 6291456 | tf_op jit(solution)/shard_map/all_to_all | solution.py:78
  110.2 6.0 %all-reduce.3.cloned.1.call-done = f32[3,3,256,512]{3,2,1,0:T(8,128)} async-done(((f32[3,3,256,512]{3,2,1,0:T(8,128)}), f32[3,3,256,512]{3,2,1,0:T(8,128)}) %all-reduce.3.cloned.1.call-update) | async-done | bytes 4718608 | tf_op jit(solution)/shard_map/psum | solution.py:83
  116.2 48.8 %all-to-all-done = bf16[3,3,256,512]{2,1,0,3:T(4,128)(2,1)S(1)} async-done(((bf16[3,3,256,512]{2,1,0,3:T(4,128)(2,1)}), bf16[3,3,256,512]{2,1,0,3:T(4,128)(2,1)S(1)}, u32[]{:S(2)}, u32[]{:S(2)}) %all-to-all-start) | async-done | bytes 2359328 | tf_op jit(solution)/shard_map/all_to_all | solution.py:78
  165.0 3.6 copy.40
  168.6 2.3 copy.59
  170.8 2.4 psum.30
  173.3 13.3 %psum.31 = f32[256]{0:T(256)S(1)} all-reduce(f32[256]{0:T(256)S(1)} %psum.30), channel_id=1, replica_groups=mesh['parts'=2,'space'=4,'filt'=2,'rep'=2] {'space'}, use_global_device_ids=true, to_apply=%region_4.0 | all-reduce | flops 256 | bytes 2048 | tf_op jit(solution)/shard_map/psum | solution.py:82
  187.2 2.5 fusion.5
  195.9 1.1 fusion.2
  197.0 1.3 copy.60
  198.3 150.8 %all-reduce.5.cloned.1.call-done = f32[3,3,256,512]{3,2,1,0:T(8,128)} async-done(((f32[3,3,256,512]{3,2,1,0:T(8,128)}), f32[3,3,256,512]{3,2,1,0:T(8,128)}) %all-reduce.5.cloned.1.call-update) | async-done | bytes 4718608 | tf_op jit(solution)/shard_map/psum | solution.py:82
  349.1 5.3 %broadcast_multiply_fusion = f32[3,3,256,512]{3,2,1,0:T(8,128)} fusion(f32[3,3,256,512]{3,2,1,0:T(8,128)} %all-reduce.5.cloned.1.call-done), kind=kLoop, calls=%fused_computation.3 | loop fusion | flops 1179648 | bytes 9437184 | tf_op jit(solution)/shard_map/mul | solution.py:87
  (62 shorter events, 21.5 us)
Async XLA Ops:
  7.2 57.7 %all-gather.3.cloned.1.call-start = ((), (), s32[]{:S(2)}) async-start(), calls=%async_computation.1 | async-start | bytes 3760128 | tf_op jit(solution)/shard_map/all_gather | solution.py:70
  8.7 7.2 %collective-permute-start.1 = (bf16[1,256,128]{1,2,0:T(8,128)(2,1)S(1)}, bf16[1,256,128]{1,2,0:T(8,128)(2,1)S(1)}, u32[]{:S(2)}, u32[]{:S(2)}) collective-permute-start(bf16[1,256,128]{1,2,0:T(8,128)(2,1)S(1)} %get-tuple-element.22), channel_id=1, source_target_pairs={{4,0},{8,4},{12,8},{5,1},{9,5},{13,9},{6,2},{10,6},{14,10},{7,3},{... | collective-permute-start | bytes 196616 | tf_op jit(solution)/shard_map/ppermute | solution.py:17
  10.0 7.5 %collective-permute-start = (bf16[1,256,128]{1,2,0:T(8,128)(2,1)S(1)}, bf16[1,256,128]{1,2,0:T(8,128)(2,1)S(1)}, u32[]{:S(2)}, u32[]{:S(2)}) collective-permute-start(bf16[1,256,128]{1,2,0:T(8,128)(2,1)S(1)} %get-tuple-element.21), channel_id=1, source_target_pairs={{0,4},{4,8},{8,12},{1,5},{5,9},{9,13},{2,6},{6,10},{10,14},{3,7},{... | collective-permute-start | bytes 196616 | tf_op jit(solution)/shard_map/ppermute | solution.py:15
  17.5 7.1 %copy-start.7 = (bf16[16,256,128]{2,1,0:T(8,128)(2,1)S(1)}, bf16[16,256,128]{2,1,0:T(8,128)(2,1)}, u32[]{:S(2)}) copy-start(bf16[16,256,128]{2,1,0:T(8,128)(2,1)} %param.7) | copy-start | bytes 3145732
  17.6 4.5 %collective-permute-start.3 = (bf16[18,256,1]{1,2,0:T(2,128)(2,1)S(1)}, bf16[18,256,1]{1,2,0:T(2,128)(2,1)S(1)}, u32[]{:S(2)}, u32[]{:S(2)}) collective-permute-start(bf16[18,256,1]{1,2,0:T(2,128)(2,1)S(1)} %get-tuple-element.18), channel_id=1, source_target_pairs={{1,0},{3,2},{5,4},{7,6},{9,8},{11,10},{13,12},{15,14},{17,16},{19,... | collective-permute-start | bytes 27656 | tf_op jit(solution)/shard_map/ppermute | solution.py:17
  19.0 3.9 %collective-permute-start.2 = (bf16[18,256,1]{1,2,0:T(2,128)(2,1)S(1)}, bf16[18,256,1]{1,2,0:T(2,128)(2,1)S(1)}, u32[]{:S(2)}, u32[]{:S(2)}) collective-permute-start(bf16[18,256,1]{1,2,0:T(2,128)(2,1)S(1)} %get-tuple-element.17), channel_id=1, source_target_pairs={{0,1},{2,3},{4,5},{6,7},{8,9},{10,11},{12,13},{14,15},{16,17},{18,... | collective-permute-start | bytes 27656 | tf_op jit(solution)/shard_map/ppermute | solution.py:15
  24.6 91.5 %all-reduce.3.cloned.1.call-start = ((), (), s32[]{:S(2)}) async-start(), calls=%async_computation.3 | async-start | bytes 9437184 | tf_op jit(solution)/shard_map/psum | solution.py:83
  25.2 48.2 %copy-start.5 = (bf16[16,256,128]{1,2,0:T(8,128)(2,1)}, bf16[16,256,128]{1,2,0:T(8,128)(2,1)S(1)}, u32[]{:S(2)}) copy-start(bf16[16,256,128]{1,2,0:T(8,128)(2,1)S(1)} %copy.38) | copy-start | bytes 3145732
  64.9 2.5 copy-start
  64.9 3.2 copy-start.2
  72.6 0.8 copy-start.8
  87.1 100.1 %all-gather.5.cloned.1.call-start = ((), (), s32[]{:S(2)}) async-start(), calls=%async_computation.2 | async-start | bytes 3760128 | tf_op jit(solution)/shard_map/all_gather | solution.py:77
  87.1 6.2 %collective-permute-start.5 = (bf16[1,256,128]{1,2,0:T(8,128)(2,1)S(1)}, bf16[1,256,128]{1,2,0:T(8,128)(2,1)S(1)}, u32[]{:S(2)}, u32[]{:S(2)}) collective-permute-start(bf16[1,256,128]{1,2,0:T(8,128)(2,1)S(1)} %get-tuple-element.20), channel_id=1, source_target_pairs={{4,0},{8,4},{12,8},{5,1},{9,5},{13,9},{6,2},{10,6},{14,10},{7,3},{... | collective-permute-start | bytes 196616 | tf_op jit(solution)/shard_map/ppermute | solution.py:17
  88.4 6.4 %collective-permute-start.4 = (bf16[1,256,128]{1,2,0:T(8,128)(2,1)S(1)}, bf16[1,256,128]{1,2,0:T(8,128)(2,1)S(1)}, u32[]{:S(2)}, u32[]{:S(2)}) collective-permute-start(bf16[1,256,128]{1,2,0:T(8,128)(2,1)S(1)} %get-tuple-element.19), channel_id=1, source_target_pairs={{0,4},{4,8},{8,12},{1,5},{5,9},{9,13},{2,6},{6,10},{10,14},{3,7},{... | collective-permute-start | bytes 196616 | tf_op jit(solution)/shard_map/ppermute | solution.py:15
  94.9 7.2 %copy-start.3 = (bf16[3,3,256,512]{3,2,1,0:T(8,128)(2,1)S(1)}, bf16[3,3,256,512]{3,2,1,0:T(8,128)(2,1)}, u32[]{:S(2)}) copy-start(bf16[3,3,256,512]{3,2,1,0:T(8,128)(2,1)} %param.5) | copy-start | bytes 7077892
  94.9 4.6 %collective-permute-start.7 = (bf16[18,256,1]{1,2,0:T(2,128)(2,1)S(1)}, bf16[18,256,1]{1,2,0:T(2,128)(2,1)S(1)}, u32[]{:S(2)}, u32[]{:S(2)}) collective-permute-start(bf16[18,256,1]{1,2,0:T(2,128)(2,1)S(1)} %get-tuple-element.16), channel_id=1, source_target_pairs={{1,0},{3,2},{5,4},{7,6},{9,8},{11,10},{13,12},{15,14},{17,16},{19,... | collective-permute-start | bytes 27656 | tf_op jit(solution)/shard_map/ppermute | solution.py:17
  96.5 3.9 %collective-permute-start.6 = (bf16[18,256,1]{1,2,0:T(2,128)(2,1)S(1)}, bf16[18,256,1]{1,2,0:T(2,128)(2,1)S(1)}, u32[]{:S(2)}, u32[]{:S(2)}) collective-permute-start(bf16[18,256,1]{1,2,0:T(2,128)(2,1)S(1)} %get-tuple-element.15), channel_id=1, source_target_pairs={{0,1},{2,3},{4,5},{6,7},{8,9},{10,11},{12,13},{14,15},{16,17},{18,... | collective-permute-start | bytes 27656 | tf_op jit(solution)/shard_map/ppermute | solution.py:15
  105.9 59.1 %all-to-all-start = ((bf16[3,3,256,512]{2,1,0,3:T(4,128)(2,1)}), bf16[3,3,256,512]{2,1,0,3:T(4,128)(2,1)S(1)}, u32[]{:S(2)}, u32[]{:S(2)}) async-start(bf16[3,3,256,512]{2,1,0,3:T(4,128)(2,1)} %copy.39), calls=%async_computation | async-start | bytes 6291456 | tf_op jit(solution)/shard_map/all_to_all | solution.py:78
  110.1 239.0 %all-reduce.5.cloned.1.call-start = ((), (), s32[]{:S(2)}) async-start(), calls=%async_computation.4 | async-start | bytes 9437184 | tf_op jit(solution)/shard_map/psum | solution.py:82
  187.2 2.5 copy-start.1
  187.2 3.2 copy-start.4
  194.7 1.2 copy-start.6
Sparse Core Ops, SparseCore 0:
  24.7 40.1 all-gather.2
  87.2 28.9 all-reduce.2
  117.7 56.2 all-gather.4
  176.2 172.7 all-reduce.4
